TPU v7x, 32 devices: a whole 2x2x4 slice. The times are simulated.
32 devices in a mesh: section: 4 (over x, core), expert: 8 (over z, y).
Axes of the slice: x: 2, y: 2, z: 4, core: 2. Of those that a mesh axis runs over, the one named last changes fastest.
Arguments:
- sent_acts: bfloat16 [4, 512, 2048], P('section', 'expert'), may hold values from -6 to 6
- stash: bfloat16 [4, 512, 2048], P('section', 'expert'), may hold values from -6 to 6
- cotangents: bfloat16 [4, 512, 2048], P('section', 'expert'), may hold values from -6 to 6
- norm_gain: bfloat16 [4, 2048], P('section'), may hold values from 0.5 to 1.5
- w_gate: bfloat16 [4, 16, 2048, 768], P('section', 'expert'), may hold values from -0.125 to 0.125
- w_up: bfloat16 [4, 16, 2048, 768], P('section', 'expert'), may hold values from -0.125 to 0.125
- w_down: bfloat16 [4, 16, 768, 2048], P('section', 'expert'), may hold values from -0.21875 to 0.21875
- routes_next: int32 [4, 512, 8], P('section', 'expert'), may hold values from 0 to 15, all different within a row; in each aligned block of 64 rows (0 to 63, 64 to 127, ..., all dimensions but the last counted through in order) at most 48 rows name the same one
- gates_next: bfloat16 [4, 512, 8], P('section', 'expert'), may hold values from 0.049804688 to 0.5
- routes_prev: int32 [4, 512, 8], P('section', 'expert'), may hold values from 0 to 15, all different within a row; in each aligned block of 64 rows (0 to 63, 64 to 127, ..., all dimensions but the last counted through in order) at most 48 rows name the same one
- gates_prev: bfloat16 [4, 512, 8], P('section', 'expert'), may hold values from 0.049804688 to 0.5
Outputs:
- fwd_out: bfloat16 [4, 512, 2048], P('section', 'expert')
- bwd_out: bfloat16 [4, 512, 2048], P('section', 'expert')
- gate_grad: bfloat16 [4, 512, 8], P('section', 'expert')
- grad_w_gate: bfloat16 [4, 16, 2048, 768], P('section', 'expert')
- grad_w_up: bfloat16 [4, 16, 2048, 768], P('section', 'expert')
- grad_w_down: bfloat16 [4, 16, 768, 2048], P('section', 'expert')
Inputs may be any that keep to these rules, and one draw needn't show every extreme that they name: `routes_next`: each row names 8 different experts. At most 48 of the 64 tokens of one device choose one expert, and in some device's tokens some expert is chosen by exactly 48. `routes_prev`: each row names 8 different experts. At most 48 of the 64 tokens of one device choose one expert, and in some device's tokens some expert is chosen by exactly 48.
All inputs are finite; a program needn't handle non-finite values.
Results may differ from a plain program's by a relative error of at most 0.008.
Values may be sent and summed in bfloat16 or wider, within the bound.
A program may use at most 128 MiB of HBM per device.

v0:
```python
import functools

import jax
import jax.numpy as jnp
from jax import lax
from jax.experimental import pallas as pl
from jax.experimental.pallas import tpu as pltpu
from jax.sharding import PartitionSpec as P

EPS = 1e-06
F32 = jnp.float32
BF16 = jnp.bfloat16
LANES = 128
VMEM = pl.BlockSpec(memory_space=pltpu.VMEM)


class Ring:
    def __init__(self, sections, owners):
        bits = owners.bit_length() - 1
        self.n = owners
        self.half = owners // 2
        self.nz = 1 << ((bits + 1) // 2)
        self.ny = owners // self.nz
        self.section = lax.axis_index("section")
        self.sections = sections
        self.me = lax.axis_index("expert")
        z, y = self.me // self.ny, self.me % self.ny
        self.place = y * self.nz + z + (y % 2) * (self.nz - 1 - 2 * z)
        self.sides = (self.owner(1), self.owner(-1))

    def owner(self, offset):
        p = (self.place + offset + self.n) % self.n
        y, r = p // self.nz, p % self.nz
        return (r + (y % 2) * (self.nz - 1 - 2 * r)) * self.ny + y

    def peer(self, offset):
        return (self.me + offset) % self.n

    def device(self, expert):
        return (self.section, expert)

    def shifted(self, by):
        return ((self.section + by + self.sections) % self.sections, self.me)

    def greet(self, sections_too):
        barrier = pltpu.get_barrier_semaphore()
        targets = [self.device(self.peer(r)) for r in range(1, self.n)]
        if sections_too:
            targets += [self.shifted(1), self.shifted(-1)]
        for target in targets:
            pl.semaphore_signal(
                barrier, inc=1, device_id=target, device_id_type=pl.DeviceIdType.MESH
            )
        pl.semaphore_wait(barrier, len(targets))


def send(src, dst, send_sem, recv_sem, device):
    return pltpu.make_async_remote_copy(
        src_ref=src,
        dst_ref=dst,
        send_sem=send_sem,
        recv_sem=recv_sem,
        device_id=device,
        device_id_type=pl.DeviceIdType.MESH,
    )


def normed(rows, gain):
    values = rows.astype(F32)
    scale = lax.rsqrt(jnp.mean(values * values, axis=-1, keepdims=True) + EPS)
    return (values * scale * gain).astype(BF16)


def dot(a, b, ca, cb):
    return lax.dot_general(a, b, (((ca,), (cb,)), ((), ())), preferred_element_type=F32)


def flat(ref):
    value = ref[...]
    return value.reshape(-1, value.shape[-1])


def tile_of(size):
    return 256 if size % 256 == 0 else LANES


def columns(i, tile):
    return pl.ds(pl.multiple_of(i * tile, tile), tile)


def gate_column(gates_ref, index):
    rows = flat(gates_ref).astype(F32)
    lane = lax.broadcasted_iota(jnp.int32, rows.shape, 1)
    return jnp.sum(jnp.where(lane == index, rows, 0.0), axis=1, keepdims=True)


def load_weights(hbm, held, sems):
    copies = [pltpu.make_async_copy(h, v, sems.at[i]) for i, (h, v) in enumerate(zip(hbm, held))]
    for copy in copies:
        copy.start()
    return copies


def gather_kernel(
    sections, owners,
    act_ref, stash_ref, cot_ref, gain_ref, dense_ref, wg_hbm, wu_hbm, wd_hbm,
    arrived_ref, next_ref, prev_ref, cots_ref, gates_ref,
    d_gate_ref, d_up_ref, gated_ref, row_ref, products_ref,
    wg, wu, wd, pre_gate, pre_up, sums,
    shift_send, shift_recv, gate_send, gate_recv, ring_send, ring_recv, weight_sem,
):
    ring = Ring(sections, owners)
    me, half = ring.me, ring.half
    tokens, width = stash_ref.shape
    local, _, units = wg.shape
    cut = width // 2
    loads = load_weights((wg_hbm, wu_hbm, wd_hbm), (wg, wu, wd), weight_sem)
    ring.greet(True)
    cot_shift = send(cot_ref, cots_ref.at[me], shift_send.at[0], shift_recv.at[0], ring.shifted(-1))
    act_shift = send(act_ref, arrived_ref, shift_send.at[1], shift_recv.at[1], ring.shifted(1))
    cot_shift.start()
    act_shift.start()
    prev_ref[me] = normed(stash_ref[...], gain_ref[...])
    gates_ref[me] = dense_ref[...]
    buffers = (prev_ref, cots_ref, next_ref)
    flying = {}

    def start(t, k):
        made = []
        for d, way in enumerate((1, -1)):
            block = ring.owner(-way * k)
            ref = buffers[t].at[block]
            if k == half - 1:
                ref = ref.at[:, pl.ds(d * cut, cut)]
            made.append(
                send(ref, ref, ring_send.at[t, d, k], ring_recv.at[t, d, k], ring.device(ring.sides[d]))
            )
        flying[t, k] = made
        for copy in made:
            copy.start()

    def arrive(t, k):
        for copy in flying[t, k]:
            copy.wait_recv()

    def advance(t, k):
        if k < half:
            arrive(t, k - 1)
            start(t, k)

    tile = tile_of(units)

    def pre_activations(j):
        @pl.loop(0, units // tile)
        def _(i):
            cols = columns(i, tile)
            rows = flat(prev_ref)
            pre_gate[j, :, cols] = dot(rows, wg[j, :, cols], 1, 0)
            pre_up[j, :, cols] = dot(rows, wu[j, :, cols], 1, 0)

    def gradients(j):
        weight = gate_column(gates_ref, (owners + me) * local + j)
        sums[j] = jnp.zeros(sums.shape[1:], F32)

        @pl.loop(0, units // tile)
        def _(i):
            cols = columns(i, tile)
            plain = dot(flat(cots_ref), wd[j, cols, :], 1, 1)
            gate, up = pre_gate[j, :, cols], pre_up[j, :, cols]
            sigma = jax.nn.sigmoid(gate)
            active = gate * sigma
            hidden = active * up
            d_hidden = weight * plain
            sums[j] += jnp.sum(hidden * plain, axis=1, keepdims=True)
            gated_ref[j, :, cols] = (weight * hidden).astype(BF16)
            d_gate_ref[j, :, cols] = (d_hidden * up * sigma * (1.0 + gate * (1.0 - sigma))).astype(BF16)
            d_up_ref[j, :, cols] = (d_hidden * active).astype(BF16)

    wide = tile_of(width)

    def row_gradients(low, high):
        @pl.loop(low, high)
        def _(i):
            cols = columns(i, wide)
            total = 0.0
            for j in range(local):
                total = total + dot(d_gate_ref[j], wg[j, cols, :], 1, 1)
                total = total + dot(d_up_ref[j], wu[j, cols, :], 1, 1)
            row_ref[:, :, cols] = total.astype(BF16).reshape(owners, tokens, wide)

    start(0, 0)
    gate_copies = [
        send(dense_ref, gates_ref.at[me], gate_send.at[r - 1], gate_recv.at[r - 1], ring.device(ring.peer(r)))
        for r in range(1, owners)
    ]
    for copy in gate_copies:
        copy.start()
    cot_shift.wait()
    start(1, 0)
    act_shift.wait()
    next_ref[me] = normed(arrived_ref[...], gain_ref[...])
    for k in range(1, half):
        advance(0, k)
        if k >= 2:
            advance(1, k - 1)
    for copy in loads:
        copy.wait()
    for copy in gate_copies:
        copy.wait()
    arrive(0, half - 1)
    start(2, 0)
    pre_activations(0)
    advance(1, half - 1)
    for j in range(1, local):
        pre_activations(j)
    advance(2, 1)
    arrive(1, half - 1)
    for j in range(local):
        gradients(j)
        advance(2, 2 + j)
    steps = list(range(2 + local, half))
    row_gradients(0, width // wide // 2)
    for k in steps:
        advance(2, k)
    row_gradients(width // wide // 2, width // wide)
    lane = lax.broadcasted_iota(jnp.int32, sums.shape[1:], 1)
    total = jnp.zeros(sums.shape[1:], F32)
    for j in range(local):
        total = jnp.where(lane == j, sums[j], total)
    products_ref[...] = total.astype(BF16).reshape(products_ref.shape)
    arrive(2, half - 1)
    for t in range(3):
        for k in range(half):
            for copy in flying[t, k]:
                copy.wait_send()


ANY = pl.BlockSpec(memory_space=pl.ANY)
VMEM_LIMIT = 60 * 2**20


def gather_call(sections, owners, act, stash, cot, gain, dense, wg, wu, wd):
    tokens, width = stash.shape
    local, _, units = wg.shape
    half = owners // 2
    every = jax.ShapeDtypeStruct((owners, tokens, width), BF16)
    inner = jax.ShapeDtypeStruct((local, owners * tokens, units), BF16)
    small = jax.ShapeDtypeStruct((owners,) + dense.shape, BF16)
    return pl.pallas_call(
        functools.partial(gather_kernel, sections, owners),
        out_shape=(
            jax.ShapeDtypeStruct((tokens, width), BF16),
            every, every, every, small, inner, inner, inner, every, small,
        ),
        in_specs=[VMEM] * 5 + [ANY] * 3,
        out_specs=(VMEM,) * 10,
        scratch_shapes=[
            pltpu.VMEM(wg.shape, BF16),
            pltpu.VMEM(wu.shape, BF16),
            pltpu.VMEM(wd.shape, BF16),
            pltpu.VMEM(inner.shape, F32),
            pltpu.VMEM(inner.shape, F32),
            pltpu.VMEM((local, owners * tokens, LANES), F32),
            pltpu.SemaphoreType.DMA((2,)),
            pltpu.SemaphoreType.DMA((2,)),
            pltpu.SemaphoreType.DMA((owners - 1,)),
            pltpu.SemaphoreType.DMA((owners - 1,)),
            pltpu.SemaphoreType.DMA((3, 2, half)),
            pltpu.SemaphoreType.DMA((3, 2, half)),
            pltpu.SemaphoreType.DMA((3,)),
        ],
        compiler_params=pltpu.CompilerParams(
            collective_id=0, has_side_effects=True, vmem_limit_bytes=VMEM_LIMIT
        ),
    )(act, stash, cot, gain, dense, wg, wu, wd)


def reduce_kernel(
    sections, owners,
    row_ref, products_ref, next_ref, prev_ref, cots_ref, gates_ref,
    d_gate_ref, d_up_ref, gated_ref, wg_hbm, wu_hbm, wd_hbm,
    summed_ref, mixed_ref, returned_ref, grad_gate_hbm, grad_up_hbm, grad_down_hbm,
    wg, wu, wd, hidden_ref, part_ref,
    outgoing, arriving, small_send, small_recv, ring_send, ring_recv, weight_sem, grad_sem,
):
    parts, totals, count = (row_ref, part_ref), (summed_ref, mixed_ref), 2
    local, _, units = wg.shape
    loads = load_weights((wg_hbm, wu_hbm, wd_hbm), (wg, wu, wd), weight_sem)
    ring = Ring(sections, owners)
    me, half = ring.me, ring.half
    width = parts[0].shape[2]
    cut = width // 2
    ring.greet(False)

    def start(t, k):
        made = []
        for d, way in enumerate((1, -1)):
            block = ring.owner(way * (half - k))
            cols = pl.ds(d * cut, cut)
            if k == 0:
                src = parts[t].at[block, :, cols]
                dst = arriving.at[t, d, k, :, cols]
            else:
                src, dst = outgoing.at[t, d, k - 1], arriving.at[t, d, k]
                if k == 1:
                    rest = pl.ds((1 - d) * cut, cut)
                    src[:, rest] = parts[t][block, :, rest]
                    src[:, cols] = (
                        parts[t][block, :, cols].astype(F32)
                        + arriving[t, d, k - 1, :, cols].astype(F32)
                    ).astype(BF16)
                else:
                    src[...] = (
                        parts[t][block].astype(F32) + arriving[t, d, k - 1].astype(F32)
                    ).astype(BF16)
            made.append(
                send(src, dst, ring_send.at[t, d, k], ring_recv.at[t, d, k], ring.device(ring.sides[d]))
            )
            made[-1].start()
        flying[t, k] = made

    flying = {}
    start(0, 0)
    small = [
        send(
            products_ref.at[ring.peer(r)], returned_ref.at[me],
            small_send.at[r - 1], small_recv.at[r - 1], ring.device(ring.peer(r)),
        )
        for r in range(1, owners)
    ]
    for copy in small:
        copy.start()
    returned_ref[me] = products_ref[me]
    def advance(t, k):
        if k < half:
            for copy in flying[t, k - 1]:
                copy.wait_recv()
            start(t, k)

    def finish(t):
        for copy in flying[t, half - 1]:
            copy.wait_recv()
        totals[t][...] = (
            parts[t][me].astype(F32)
            + arriving[t, 0, half - 1].astype(F32)
            + arriving[t, 1, half - 1].astype(F32)
        )

    tile, wide = tile_of(units), tile_of(width)

    def hidden(j):
        weight = gate_column(gates_ref, me * local + j)

        @pl.loop(0, units // tile)
        def _(i):
            cols = columns(i, tile)
            rows = flat(next_ref)
            gate = dot(rows, wg[j, :, cols], 1, 0)
            up = dot(rows, wu[j, :, cols], 1, 0)
            hidden_ref[j, :, cols] = (weight * (gate * jax.nn.sigmoid(gate) * up)).astype(BF16)

    def mix(low, high):
        @pl.loop(low, high)
        def _(i):
            cols = columns(i, wide)
            total = 0.0
            for j in range(local):
                total = total + dot(hidden_ref[j], wd[j, :, cols], 1, 0)
            part_ref[:, :, cols] = total.astype(BF16).reshape(part_ref.shape[:2] + (wide,))

    grads = []

    def weight_gradient(held, out_hbm, index, j):
        rows_size = held.shape[1]
        step = tile_of(rows_size)

        @pl.loop(0, rows_size // step)
        def _(i):
            rows = columns(i, step)
            if index == 2:
                left, right = gated_ref[j, :, rows], flat(cots_ref)
            else:
                left = prev_ref[:, :, rows].reshape(-1, step)
                right = (d_gate_ref, d_up_ref)[index][j]
            held[j, rows, :] = dot(left, right, 0, 0).astype(BF16)

        copy = pltpu.make_async_copy(held.at[j], out_hbm.at[j], grad_sem.at[index, j])
        copy.start()
        grads.append(copy)

    for copy in loads:
        copy.wait()
    for j in range(local):
        hidden(j)
        advance(0, 1 + j)
    mix(0, width // wide // 2)
    for k in range(1 + local, half):
        advance(0, k)
    mix(width // wide // 2, width // wide)
    start(1, 0)
    finish(0)
    k = 1
    for index, (held, out) in enumerate(((wg, grad_gate_hbm), (wu, grad_up_hbm), (wd, grad_down_hbm))):
        for j in range(local):
            weight_gradient(held, out, index, j)
            advance(1, k)
            k += 1
    for k in range(k, half):
        advance(1, k)
    finish(1)
    for copy in grads:
        copy.wait()
    for t in range(count):
        for k in range(half):
            for copy in flying[t, k]:
                copy.wait_send()
    for copy in small:
        copy.wait()


def reduce_call(sections, owners, row, products, rows_next, prev, cots, gates, inner, weights):
    _, tokens, width = row.shape
    half = owners // 2
    total = jax.ShapeDtypeStruct((tokens, width), F32)
    return pl.pallas_call(
        functools.partial(reduce_kernel, sections, owners),
        out_shape=(total, total, jax.ShapeDtypeStruct(products.shape, BF16))
        + tuple(jax.ShapeDtypeStruct(w.shape, BF16) for w in weights),
        in_specs=[VMEM] * 9 + [ANY] * 3,
        out_specs=(VMEM,) * 3 + (ANY,) * 3,
        scratch_shapes=[pltpu.VMEM(w.shape, BF16) for w in weights]
        + [
            pltpu.VMEM(inner[0].shape, BF16),
            pltpu.VMEM(row.shape, BF16),
            pltpu.VMEM((2, 2, half - 1, tokens, width), BF16),
            pltpu.VMEM((2, 2, half, tokens, width), BF16),
            pltpu.SemaphoreType.DMA((owners - 1,)),
            pltpu.SemaphoreType.DMA((owners - 1,)),
            pltpu.SemaphoreType.DMA((2, 2, half)),
            pltpu.SemaphoreType.DMA((2, 2, half)),
            pltpu.SemaphoreType.DMA((3,)),
            pltpu.SemaphoreType.DMA((3, weights[0].shape[0])),
        ],
        compiler_params=pltpu.CompilerParams(
            collective_id=1, has_side_effects=True, vmem_limit_bytes=VMEM_LIMIT
        ),
    )(row, products, rows_next, prev, cots, gates, *inner, *weights)


def apply_rms_norm(rows, gain):
    values = rows.astype(F32)
    scale = lax.rsqrt(jnp.mean(values * values, axis=-1, keepdims=True) + EPS)
    unit = values * scale
    return (unit * gain).astype(BF16), unit, scale


def dense_gates(routes, gates, experts_all):
    hit = routes[:, :, None] == jnp.arange(experts_all, dtype=jnp.int32)
    return jnp.sum(jnp.where(hit, gates.astype(F32)[:, :, None], 0.0), axis=1).astype(BF16)


def per_device(
    sent_acts,
    stash,
    cotangents,
    norm_gain,
    w_gate,
    w_up,
    w_down,
    routes_next,
    gates_next,
    routes_prev,
    gates_prev,
):
    owners = lax.axis_size("expert")
    me = lax.axis_index("expert")
    gain = norm_gain[0].astype(F32)
    wg, wu, wd = w_gate[0], w_up[0], w_down[0]
    local, width, hidden_units = wg.shape
    experts_all = local * owners
    tokens = stash.shape[1]

    dense = jnp.concatenate(
        [
            dense_gates(routes_next[0], gates_next[0], experts_all),
            dense_gates(routes_prev[0], gates_prev[0], experts_all),
        ],
        axis=1,
    )
    dense = jnp.pad(dense, ((0, 0), (0, LANES - dense.shape[1])))
    sections = lax.axis_size("section")
    _, unit_rows, scale = apply_rms_norm(stash[0], gain)
    weights = (wg, wu, wd)
    arrived, next_all, prev_all, cot_all, dense_all, d_gate, d_up, gated, row, products = gather_call(
        sections, owners, sent_acts[0], stash[0], cotangents[0], gain[None], dense, *weights
    )
    cot = lax.dynamic_index_in_dim(cot_all, me, 0, keepdims=False)
    summed, mixed, products_back, grad_gate, grad_up, grad_down = reduce_call(
        sections, owners, row, products, next_all, prev_all, cot_all, dense_all,
        (d_gate, d_up, gated), weights,
    )
    products_back = products_back[:, :, :local]

    fwd_out = (arrived.astype(F32) + mixed).astype(BF16)

    by_expert = jnp.transpose(products_back, (1, 0, 2)).reshape(tokens, experts_all).astype(F32)
    hit = routes_prev[0][:, :, None] == jnp.arange(experts_all, dtype=jnp.int32)
    gate_grad = jnp.sum(jnp.where(hit, by_expert[:, None, :], 0.0), axis=-1).astype(BF16)

    normalized_gradient = summed * gain
    backward = cot.astype(F32) + scale * (
        normalized_gradient
        - unit_rows * jnp.mean(normalized_gradient * unit_rows, axis=-1, keepdims=True)
    )
    return (
        fwd_out[None],
        backward.astype(BF16)[None],
        gate_grad[None],
        grad_gate[None],
        grad_up[None],
        grad_down[None],
    )


def solution(mesh):
    tokens = P("section", "expert", None)
    weights = P("section", "expert", None, None)
    return jax.shard_map(
        per_device,
        mesh=mesh,
        in_specs=(tokens, tokens, tokens, P("section", None), weights, weights, weights)
        + (tokens,) * 4,
        out_specs=(tokens, tokens, tokens, weights, weights, weights),
        check_vma=False,
    )
```

profile of v0, /device:TPU:0, one launch (start us, length us, event | category | flops | bytes accessed | tf_op | source)
XLA Modules:
  0.0 173.2 jit_solution(7672447729320310629)
XLA Ops:
  0.6 0.7 bitcast_convert_fusion
  1.3 0.7 select_reduce_fusion.1
  2.0 0.1 copy.31
  2.1 0.7 bitcast_convert_fusion.1
  2.8 0.7 select_reduce_fusion.2
  3.5 0.1 copy.30
  3.6 0.7 fusion.12.dense_ref
  4.3 1.3 convert_element_type.76.gain_ref
  5.6 84.1 %shard_map.154 = (bf16[64,2048]{1,0:T(8,128)(2,1)}, bf16[8,64,2048]{2,1,0:T(8,128)(2,1)}, bf16[8,64,2048]{2,1,0:T(8,128)(2,1)}, bf16[8,64,2048]{2,1,0:T(8,128)(2...) custom-call(bf16[64,2048]{1,0:T(8,128)(2,1)} %bitcast.48, ...), custom_call_target="tpu_custom_call" | custom-call | tf_op jit(solution)/shard_map/pallas_call | solution.py:249
  89.7 0.0 copy-start
  89.7 0.0 copy-start.2
  89.7 0.0 copy-start.1
  89.7 0.0 copy-start.3
  89.7 65.3 %shard_map.155 = (f32[64,2048]{1,0:T(8,128)}, f32[64,2048]{1,0:T(8,128)}, bf16[8,64,128]{2,1,0:T(8,128)(2,1)}, bf16[2,2048,768]{2,1,0:T(8,128)(2,1)}, bf16[2,204...) custom-call(bf16[8,64,2048]{2,1,0:T(8,128)(2,1)} %get-tuple-element.23.row_ref, ...), custom_call_target="tpu_custom_call" | custom-call | tf_op jit(solution)/shard_map/pallas_call | solution.py:425
  155.1 0.0 copy-done
  155.1 0.2 fusion.7
  155.2 0.0 copy-done.2
  155.2 1.3 fusion.2
  156.5 0.0 copy-done.1
  156.5 0.0 slice-start.2
  156.6 2.4 %fusion.8 = (bf16[1,64,2048]{2,1,0:T(8,128)(2,1)}, bf16[1,64,2048]{2,1,0:T(8,128)(2,1)}) fusion(f32[64,2048]{1,0:T(8,128)} %get-tuple-element.32, bf16[64,2048]{1,0:T(8,128)(2,1)S(1)} %copy-done.1, f32[64]{0:T(128)S(1)} %broadcast_multiply_fusion, bf16[1,64,2048]{2,1,0:T(8,128)(2,1)S(1)} %copy-done, f32[64,2048]{1,0:T(8,128)} %get-tuple-element.33, ...), kind=kLoop, calls=%fused_computation.11 | loop fusion | flops 1572864 | bytes 2368004 | tf_op jit(solution)/shard_map/broadcast_in_dim | solution.py:516
  159.0 0.9 convert_bitcast_fusion
  159.9 0.1 copy.32
  160.0 0.0 copy-done.3
  160.0 0.6 select_reduce_fusion
  160.7 6.5 %copy.36 = bf16[1,2,2048,768]{3,2,1,0:T(8,128)(2,1)} copy(bf16[1,2,2048,768]{3,2,1,0:T(8,128)(2,1)} %bitcast.46) | data formatting | bytes 12582912
  167.2 0.0 slice-done.2
  167.2 0.0 slice-done.3
  167.2 2.8 %copy.37 = bf16[1,2,2048,768]{3,2,1,0:T(8,128)(2,1)} copy(bf16[1,2,2048,768]{3,2,1,0:T(8,128)(2,1)S(1)} %bitcast.45) | data formatting | bytes 12582912
  170.0 0.0 slice-done
  170.0 0.5 slice-done.1
  170.5 2.7 %copy.38 = bf16[1,2,768,2048]{3,2,1,0:T(8,128)(2,1)} copy(bf16[1,2,768,2048]{3,2,1,0:T(8,128)(2,1)S(1)} %bitcast.42) | data formatting | bytes 12582912
  (7 shorter events, 0.0 us)
Async XLA Ops:
  89.7 65.4 %copy-start = (bf16[1,64,2048]{2,1,0:T(8,128)(2,1)S(1)}, bf16[1,64,2048]{2,1,0:T(8,128)(2,1)}, u32[]{:S(2)}) copy-start(bf16[1,64,2048]{2,1,0:T(8,128)(2,1)} %param.12) | copy-start | bytes 786436
  89.7 65.5 %copy-start.2 = (f32[1,2048]{1,0:T(1,128)S(1)}, f32[1,2048]{1,0:T(1,128)}, u32[]{:S(2)}) copy-start(f32[1,2048]{1,0:T(1,128)} %convert_element_type.76.gain_ref) | copy-start | bytes 24580
  89.7 66.8 %copy-start.1 = (bf16[64,2048]{1,0:T(8,128)(2,1)S(1)}, bf16[64,2048]{1,0:T(8,128)(2,1)}, u32[]{:S(2)}) copy-start(bf16[64,2048]{1,0:T(8,128)(2,1)} %get-tuple-element.22) | copy-start | bytes 786436
  89.7 70.3 %copy-start.3 = (s32[1,64,8]{1,2,0:T(8,128)S(1)}, s32[1,64,8]{1,2,0:T(8,128)}, u32[]{:S(2)}) copy-start(s32[1,64,8]{1,2,0:T(8,128)} %param.20) | copy-start | bytes 6148
  156.5 10.7 %slice-start.2 = ((s8[6291456]{0:T(1024)(128)(4,1)}), s8[2097152]{0:T(1024)(128)(4,1)S(1)}, s32[]{:S(2)}) async-start(s8[6291456]{0:T(1024)(128)(4,1)} %bitcast.43), calls=%async_computation.2 | async-start | bytes 4194304
  160.7 6.5 %slice-start.3 = ((s8[6291456]{0:T(1024)(128)(4,1)}), s8[4194304]{0:T(1024)(128)(4,1)S(1)}, s32[]{:S(2)}) async-start(s8[6291456]{0:T(1024)(128)(4,1)} %bitcast.43), calls=%async_computation.3 | async-start | bytes 8388608
  160.7 9.4 %slice-start = ((s8[6291456]{0:T(1024)(128)(4,1)}), s8[4194304]{0:T(1024)(128)(4,1)S(1)}, s32[]{:S(2)}) async-start(s8[6291456]{0:T(1024)(128)(4,1)} %bitcast.40), calls=%async_computation | async-start | bytes 8388608
  167.2 3.3 %slice-start.1 = ((s8[6291456]{0:T(1024)(128)(4,1)}), s8[2097152]{0:T(1024)(128)(4,1)S(1)}, s32[]{:S(2)}) async-start(s8[6291456]{0:T(1024)(128)(4,1)} %bitcast.40), calls=%async_computation.1 | async-start | bytes 4194304
where the time goes:
time: 174 us; the launch traced here: 173 us
  Pallas kernels  149 us (86%)
  local copies, waits for them, and re-layouts  12.9 us (7%)
  other arithmetic  10.2 us (6%)
    pallas_call x1, Pallas kernels, gather_call(): pl.pallas_call(functools.partial(gather_kernel, sections, owners), out_sh...  84.1 us
    pallas_call x1, Pallas kernels, reduce_call(): pl.pallas_call(functools.partial(reduce_kernel, sections, owners), out_sh...  65.3 us
    unnamed x19, local copies, waits for them, and re-layouts  12.5 us

commit v1 on v0

--- a/solution.py
+++ b/solution.py
@@ -203,12 +203,12 @@
         advance(0, k)
         if k >= 2:
             advance(1, k - 1)
+    start(2, 0)
     for copy in loads:
         copy.wait()
     for copy in gate_copies:
         copy.wait()
     arrive(0, half - 1)
-    start(2, 0)
     pre_activations(0)
     advance(1, half - 1)
     for j in range(1, local):
@@ -392,21 +392,22 @@
         copy.wait()
     for j in range(local):
         hidden(j)
-        advance(0, 1 + j)
-    mix(0, width // wide // 2)
-    for k in range(1 + local, half):
-        advance(0, k)
-    mix(width // wide // 2, width // wide)
+    advance(0, 1)
+    mix(0, width // wide)
     start(1, 0)
-    finish(0)
-    k = 1
+    advance(0, 2)
+    hops = []
+    for k in range(1, half):
+        hops += [(1, k), (0, k + 2)]
+    hops = [(t, k) for t, k in hops if k < half]
     for index, (held, out) in enumerate(((wg, grad_gate_hbm), (wu, grad_up_hbm), (wd, grad_down_hbm))):
         for j in range(local):
             weight_gradient(held, out, index, j)
-            advance(1, k)
-            k += 1
-    for k in range(k, half):
-        advance(1, k)
+            if hops:
+                advance(*hops.pop(0))
+    for hop in hops:
+        advance(*hop)
+    finish(0)
     finish(1)
     for copy in grads:
         copy.wait()

time: 174 us -> 168 us (0.966)
  Pallas kernels: 149 us -> 144 us
    pallas_call x1, Pallas kernels: 65.3 us -> 59.5 us  [reduce_call(): pl.pallas_call(functools.partial(reduce_kernel, sections, owners), out_sh...]
where the time goes in v1:
time: 168 us; the launch traced here: 167 us
  Pallas kernels  144 us (86%)
  local copies, waits for them, and re-layouts  12.9 us (8%)
  other arithmetic  10.2 us (6%)
    pallas_call x1, Pallas kernels, gather_call(): pl.pallas_call(functools.partial(gather_kernel, sections, owners), out_sh...  84.1 us
    pallas_call x1, Pallas kernels, reduce_call(): pl.pallas_call(functools.partial(reduce_kernel, sections, owners), out_sh...  59.5 us
    unnamed x19, local copies, waits for them, and re-layouts  12.5 us

profile of v1, /device:TPU:0, one launch (start us, length us, event | category | flops | bytes accessed | tf_op | source)
XLA Modules:
  0.0 167.4 jit_solution(2777363204694695845)
XLA Ops:
  0.6 0.7 bitcast_convert_fusion
  1.3 0.7 select_reduce_fusion.1
  2.0 0.1 copy.31
  2.1 0.7 bitcast_convert_fusion.1
  2.8 0.7 select_reduce_fusion.2
  3.5 0.1 copy.30
  3.6 0.7 fusion.12.dense_ref
  4.3 1.3 convert_element_type.76.gain_ref
  5.6 84.1 %shard_map.154 = (bf16[64,2048]{1,0:T(8,128)(2,1)}, bf16[8,64,2048]{2,1,0:T(8,128)(2,1)}, bf16[8,64,2048]{2,1,0:T(8,128)(2,1)}, bf16[8,64,2048]{2,1,0:T(8,128)(2...) custom-call(bf16[64,2048]{1,0:T(8,128)(2,1)} %bitcast.48, ...), custom_call_target="tpu_custom_call" | custom-call | tf_op jit(solution)/shard_map/pallas_call | solution.py:249
  89.7 0.0 copy-start
  89.7 0.0 copy-start.2
  89.7 0.0 copy-start.1
  89.7 0.0 copy-start.3
  89.7 59.5 %shard_map.155 = (f32[64,2048]{1,0:T(8,128)}, f32[64,2048]{1,0:T(8,128)}, bf16[8,64,128]{2,1,0:T(8,128)(2,1)}, bf16[2,2048,768]{2,1,0:T(8,128)(2,1)}, bf16[2,204...) custom-call(bf16[8,64,2048]{2,1,0:T(8,128)(2,1)} %get-tuple-element.23.row_ref, ...), custom_call_target="tpu_custom_call" | custom-call | tf_op jit(solution)/shard_map/pallas_call | solution.py:426
  149.3 0.0 copy-done
  149.3 0.2 fusion.7
  149.5 0.0 copy-done.2
  149.5 1.3 fusion.2
  150.8 0.0 copy-done.1
  150.8 0.0 slice-start.2
  150.8 2.4 %fusion.8 = (bf16[1,64,2048]{2,1,0:T(8,128)(2,1)}, bf16[1,64,2048]{2,1,0:T(8,128)(2,1)}) fusion(f32[64,2048]{1,0:T(8,128)} %get-tuple-element.32, bf16[64,2048]{1,0:T(8,128)(2,1)S(1)} %copy-done.1, f32[64]{0:T(128)S(1)} %broadcast_multiply_fusion, bf16[1,64,2048]{2,1,0:T(8,128)(2,1)S(1)} %copy-done, f32[64,2048]{1,0:T(8,128)} %get-tuple-element.33, ...), kind=kLoop, calls=%fused_computation.11 | loop fusion | flops 1572864 | bytes 2368004 | tf_op jit(solution)/shard_map/broadcast_in_dim | solution.py:517
  153.2 0.9 convert_bitcast_fusion
  154.1 0.1 copy.32
  154.3 0.0 copy-done.3
  154.3 0.6 select_reduce_fusion
  154.9 6.5 %copy.36 = bf16[1,2,2048,768]{3,2,1,0:T(8,128)(2,1)} copy(bf16[1,2,2048,768]{3,2,1,0:T(8,128)(2,1)} %bitcast.46) | data formatting | bytes 12582912
  161.4 0.0 slice-done.2
  161.4 0.0 slice-done.3
  161.4 2.8 %copy.37 = bf16[1,2,2048,768]{3,2,1,0:T(8,128)(2,1)} copy(bf16[1,2,2048,768]{3,2,1,0:T(8,128)(2,1)S(1)} %bitcast.45) | data formatting | bytes 12582912
  164.2 0.0 slice-done
  164.2 0.5 slice-done.1
  164.7 2.7 %copy.38 = bf16[1,2,768,2048]{3,2,1,0:T(8,128)(2,1)} copy(bf16[1,2,768,2048]{3,2,1,0:T(8,128)(2,1)S(1)} %bitcast.42) | data formatting | bytes 12582912
  (7 shorter events, 0.0 us)
Async XLA Ops:
  89.7 59.6 %copy-start = (bf16[1,64,2048]{2,1,0:T(8,128)(2,1)S(1)}, bf16[1,64,2048]{2,1,0:T(8,128)(2,1)}, u32[]{:S(2)}) copy-start(bf16[1,64,2048]{2,1,0:T(8,128)(2,1)} %param.12) | copy-start | bytes 786436
  89.7 59.8 %copy-start.2 = (f32[1,2048]{1,0:T(1,128)S(1)}, f32[1,2048]{1,0:T(1,128)}, u32[]{:S(2)}) copy-start(f32[1,2048]{1,0:T(1,128)} %convert_element_type.76.gain_ref) | copy-start | bytes 24580
  89.7 61.1 %copy-start.1 = (bf16[64,2048]{1,0:T(8,128)(2,1)S(1)}, bf16[64,2048]{1,0:T(8,128)(2,1)}, u32[]{:S(2)}) copy-start(bf16[64,2048]{1,0:T(8,128)(2,1)} %get-tuple-element.22) | copy-start | bytes 786436
  89.7 64.5 %copy-start.3 = (s32[1,64,8]{1,2,0:T(8,128)S(1)}, s32[1,64,8]{1,2,0:T(8,128)}, u32[]{:S(2)}) copy-start(s32[1,64,8]{1,2,0:T(8,128)} %param.20) | copy-start | bytes 6148
  150.8 10.7 %slice-start.2 = ((s8[6291456]{0:T(1024)(128)(4,1)}), s8[2097152]{0:T(1024)(128)(4,1)S(1)}, s32[]{:S(2)}) async-start(s8[6291456]{0:T(1024)(128)(4,1)} %bitcast.43), calls=%async_computation.2 | async-start | bytes 4194304
  154.9 6.5 %slice-start.3 = ((s8[6291456]{0:T(1024)(128)(4,1)}), s8[4194304]{0:T(1024)(128)(4,1)S(1)}, s32[]{:S(2)}) async-start(s8[6291456]{0:T(1024)(128)(4,1)} %bitcast.43), calls=%async_computation.3 | async-start | bytes 8388608
  154.9 9.4 %slice-start = ((s8[6291456]{0:T(1024)(128)(4,1)}), s8[4194304]{0:T(1024)(128)(4,1)S(1)}, s32[]{:S(2)}) async-start(s8[6291456]{0:T(1024)(128)(4,1)} %bitcast.40), calls=%async_computation | async-start | bytes 8388608
  161.4 3.3 %slice-start.1 = ((s8[6291456]{0:T(1024)(128)(4,1)}), s8[2097152]{0:T(1024)(128)(4,1)S(1)}, s32[]{:S(2)}) async-start(s8[6291456]{0:T(1024)(128)(4,1)} %bitcast.40), calls=%async_computation.1 | async-start | bytes 4194304
